TPU v7x, 32 devices: a whole 2x2x4 slice. The times are simulated.
32 devices in a mesh: row: 8 (over y, x, core), col: 4 (over z).
Axes of the slice: x: 2, y: 2, z: 4, core: 2. Of those that a mesh axis runs over, the one named last changes fastest.
Arguments:
- density: bfloat16 [4096, 4096], P('row', 'col'), as said below
- pattern: int32 [64, 64], P('row', 'col'), may hold values from 0 to 1, as said below
Outputs:
- updated: bfloat16 [4096, 4096], P('row', 'col')
- occupations: float32 [2], replicated
Inputs may be any that keep to these rules, and one draw needn't show every extreme that they name: pattern is symmetric, every diagonal block is 1. density is exactly symmetric and zero wherever pattern is 0.
All inputs are finite; a program needn't handle non-finite values.
Results may differ from a plain program's by a relative error of at most 0.0015.
Values may be sent and summed in bfloat16 or wider, within the bound.
A program may use at most 64 MiB of HBM per device.

v0:
```python
import jax
import jax.numpy as jnp
from jax import lax
from jax.sharding import PartitionSpec as P

BLK = 64


def expand_blocks(block_mask, width):
    block_rows, block_cols = block_mask.shape
    grid = jnp.broadcast_to(
        block_mask.astype(jnp.float32)[:, None, :, None], (block_rows, width, block_cols, width)
    )
    return grid.reshape(block_rows * width, block_cols * width)


def body(density, pattern):
    slab_rows, slab_cols = density.shape
    cell_mask = expand_blocks(pattern, BLK)
    column_panel = lax.all_gather(density, "row", axis=0, tiled=True)
    row_offset = lax.axis_index("row") * slab_rows
    col_offset = lax.axis_index("col") * slab_cols
    global_rows = row_offset + lax.iota(jnp.int32, slab_rows)
    global_cols = col_offset + lax.iota(jnp.int32, slab_cols)
    on_diagonal = global_rows[:, None] == global_cols[None, :]
    density_wide = density.astype(jnp.float32)
    trace_p_part = jnp.sum(jnp.where(on_diagonal, density_wide, 0.0))
    square = jnp.dot(
        lax.all_gather(density, "col", axis=1, tiled=True),
        column_panel,
        preferred_element_type=jnp.float32,
    )
    square = square * cell_mask
    trace_c_part = jnp.sum(jnp.where(on_diagonal, square, 0.0))
    trace_p, trace_c = lax.psum((trace_p_part, trace_c_part), ("row", "col"))
    order_total = slab_rows * lax.axis_size("row")
    take_square = trace_p > 1.0 * order_total
    updated = jnp.where(take_square, square, cell_mask * (2.0 * density_wide - square))
    trace_new = jnp.where(take_square, trace_c, 2.0 * trace_p - trace_c)
    occupations = jnp.stack([trace_p, trace_new]) / order_total
    return (updated.astype(jnp.bfloat16), occupations)


def solution(mesh):
    placed = (P("row", "col"), P("row", "col"))
    return jax.shard_map(
        body, mesh=mesh, in_specs=placed, out_specs=(P("row", "col"), P()), check_vma=False
    )
```

profile of v0, /device:TPU:0, one launch (start us, length us, event | category | flops | bytes accessed | tf_op | source)
XLA Modules:
  0.0 212.4 jit_solution(5599611315656936817)
XLA Ops:
  7.2 0.0 copy-start.1
  7.2 0.0 all-gather.3.cloned.1.call-start
  7.2 0.7 all-gather.3.cloned.1.call-update
  7.9 0.0 all-gather.5.cloned.1.call-start
  8.0 0.7 all-gather.5.cloned.1.call-update
  8.7 0.0 copy-done.1
  8.7 2.3 %broadcast_in_dim.14 = f32[8,64,16,64]{3,2,1,0:T(8,128)} broadcast(f32[8,16]{1,0:T(8,128)S(1)} %convert_element_type.10), dimensions={0,2} | broadcast | bytes 2097664 | tf_op jit(solution)/shard_map/broadcast_in_dim | solution.py:11
  11.0 0.0 copy-start
  11.0 3.6 %reshape.16 = f32[512,1024]{1,0:T(8,128)S(1)} reshape(f32[8,64,16,64]{3,2,1,0:T(8,128)} %broadcast_in_dim.14) | data formatting | bytes 4194304 | tf_op jit(solution)/shard_map/reshape | solution.py:14
  14.6 78.5 %all-gather.3.cloned.1.call-done = bf16[512,4096]{1,0:T(8,128)(2,1)} async-done(((bf16[512,1024]{1,0:T(8,128)(2,1)}), bf16[512,4096]{1,0:T(8,128)(2,1)}) %all-gather.3.cloned.1.call-update) | async-done | bytes 4194320 | tf_op jit(solution)/shard_map/all_gather | solution.py:29
  93.1 54.8 %all-gather.5.cloned.1.call-done = bf16[4096,1024]{1,0:T(8,128)(2,1)} async-done(((bf16[512,1024]{1,0:T(8,128)(2,1)}), bf16[4096,1024]{1,0:T(8,128)(2,1)}) %all-gather.5.cloned.1.call-update) | async-done | bytes 8388624 | tf_op jit(solution)/shard_map/all_gather | solution.py:20
  147.9 0.0 copy-done
  147.9 11.1 %fusion.5 = (f32[]{:T(128)}, f32[]{:T(128)}, f32[512,1024]{1,0:T(8,128)}) fusion(f32[512,1024]{1,0:T(8,128)S(1)} %reshape.16, s32[1024]{0:T(1024)S(1)} %iota_add_fusion, s32[512]{0:T(512)S(1)} %iota_add_fusion.1, bf16[512,1024]{1,0:T(8,128)(2,1)S(1)} %copy-done, bf16[512,4096]{1,0:T(8,128)(2,1)} %all-gather.3.cloned.1.call-done, ...), kind=kOutput, calls=%fused_computation.8 | convolution fusion | flops 4298637312 | bytes 17831944 | tf_op jit(solution)/shard_map/dot_general | solution.py:28
  159.0 39.6 %all-reduce = (f32[]{:T(128)}, f32[]{:T(128)}) all-reduce(f32[]{:T(128)} %get-tuple-element.3, f32[]{:T(128)} %get-tuple-element.2), channel_id=1, replica_groups=mesh['row'=8,'col'=4] {'row','col'}, use_global_device_ids=true, to_apply=%region_1.2 | all-reduce | flops 2 | bytes 16 | tf_op jit(solution)/shard_map/psum | solution.py:35
  201.2 3.2 %fusion.3 = bf16[512,1024]{1,0:T(8,128)(2,1)} fusion(f32[512,1024]{1,0:T(8,128)S(1)} %reshape.16, bf16[512,1024]{1,0:T(8,128)(2,1)S(1)} %copy-done, f32[512,1024]{1,0:T(8,128)} %get-tuple-element.6, pred[]{:T(512)S(6)} %gt.3), kind=kLoop, calls=%fused_computation.6 | loop fusion | flops 3670016 | bytes 6291457 | tf_op jit(solution)/shard_map/convert_element_type | solution.py:41
  204.3 1.2 maximum_multiply_fusion
  (3 shorter events, 0.0 us)
Async XLA Ops:
  7.2 1.5 copy-start.1
  7.2 85.9 %all-gather.3.cloned.1.call-start = ((), (), s32[]{:S(2)}) async-start(), calls=%async_computation | async-start | bytes 5242880 | tf_op jit(solution)/shard_map/all_gather | solution.py:29
  7.9 140.0 %all-gather.5.cloned.1.call-start = ((), (), s32[]{:S(2)}) async-start(), calls=%async_computation.1 | async-start | bytes 9437184 | tf_op jit(solution)/shard_map/all_gather | solution.py:20
  11.0 136.9 %copy-start = (bf16[512,1024]{1,0:T(8,128)(2,1)S(1)}, bf16[512,1024]{1,0:T(8,128)(2,1)}, u32[]{:S(2)}) copy-start(bf16[512,1024]{1,0:T(8,128)(2,1)} %param.2) | copy-start | bytes 3145732
Sparse Core Ops, SparseCore 0:
  9.6 83.4 all-gather.2
  95.0 52.9 all-gather.4
where the time goes:
time: 213 us; the launch traced here: 212 us
  waiting for transfers between devices  135 us (63%)
  blocking collectives  39.6 us (19%)
  between operations  16.7 us (8%)
  matrix products  11.1 us (5%)
  local copies, waits for them, and re-layouts  5.88 us (3%)
  other arithmetic  4.4 us (2%)
    all_gather x1, waiting for transfers between devices, body(): lax.all_gather(density, 'col', axis=1, tiled=True)  78.5 us
    all_gather x1, waiting for transfers between devices, body(): column_panel = lax.all_gather(density, 'row', axis=0, tiled=True)  54.8 us
    psum x1, blocking collectives, body(): trace_p, trace_c = lax.psum((trace_p_part, trace_c_part), ('row', 'col'))  39.6 us
    dot_general x1, matrix products, body(): jnp.dot(lax.all_gather(density, 'col', axis=1, tiled=True), column_panel,...  11.1 us
  transfers between devices with their start and end apart: 2, of which 2 were waited for; matrix products, arithmetic and copies ran while one was open for 3% of the time, Pallas kernels for 0%

commit v1 on v0

--- a/solution.py
+++ b/solution.py
@@ -4,6 +4,27 @@
 from jax.sharding import PartitionSpec as P
 
 BLK = 64
+
+
+def find_shapes(my_tile, array_dim):
+    my_tile = jnp.moveaxis(my_tile, 0, array_dim)
+    a_next = my_tile.shape
+    return my_tile.reshape(
+        *a_next[:array_dim], a_next[array_dim] * a_next[array_dim + 1], *a_next[array_dim + 2 :]
+    )
+
+
+def _press_table(vector, across):
+    local_out = lax.axis_size(across)
+    oldest, k_now = (local_out, lax.axis_index(across))
+    y2, mid_arr = (vector[None], 1)
+    while mid_arr < oldest:
+        right_arr = tuple(((dev, dev ^ mid_arr) for dev in range(oldest)))
+        all_values = lax.ppermute(y2, across, right_arr)
+        r_now = k_now & mid_arr == 0
+        y2 = jnp.concatenate([jnp.where(r_now, y2, all_values), jnp.where(r_now, all_values, y2)])
+        mid_arr *= 2
+    return y2
 
 
 def expand_blocks(block_mask, width):
@@ -25,10 +46,12 @@
     on_diagonal = global_rows[:, None] == global_cols[None, :]
     density_wide = density.astype(jnp.float32)
     trace_p_part = jnp.sum(jnp.where(on_diagonal, density_wide, 0.0))
+
+    def bind_clusters(xs, inner_x, dimension_no):
+        return find_shapes(_press_table(xs, inner_x), dimension_no)
+
     square = jnp.dot(
-        lax.all_gather(density, "col", axis=1, tiled=True),
-        column_panel,
-        preferred_element_type=jnp.float32,
+        bind_clusters(density, "col", 1), column_panel, preferred_element_type=jnp.float32
     )
     square = square * cell_mask
     trace_c_part = jnp.sum(jnp.where(on_diagonal, square, 0.0))

time: 213 us -> 202 us (0.948)
  waiting for transfers between devices: 135 us -> 107 us
  other arithmetic: 4.4 us -> 11.5 us
  starting transfers between devices: 0.08 us -> 5.88 us
  local copies, waits for them, and re-layouts: 5.88 us -> 9.49 us
    ppermute x0 -> x2, waiting for transfers between devices: none -> 106 us  [_press_table(): all_values = lax.ppermute(y2, across, right_arr)]
    all_gather x1 -> x0, waiting for transfers between devices: 78.5 us -> none  [body(): lax.all_gather(density, 'col', axis=1, tiled=True)]
    all_gather x1, waiting for transfers between devices: 54.8 us -> 0.01 us  [body(): column_panel = lax.all_gather(density, 'row', axis=0, tiled=True)]
    ppermute x0 -> x2, starting transfers between devices: none -> 5.84 us  [_press_table(): all_values = lax.ppermute(y2, across, right_arr)]
    concatenate x0 -> x2, other arithmetic: none -> 3.93 us  [_press_table(): jnp.concatenate([jnp.where(r_now, y2, all_values), jnp.where(r_now, all_v...]
    select_n x0 -> x2, other arithmetic: none -> 3.23 us  [_press_table(): jnp.where(r_now, y2, all_values)]
    unnamed x4 -> x7, local copies, waits for them, and re-layouts: 0.01 us -> 2.35 us
  transfers between devices with their start and end apart: 2 -> 3, of which waited for: 2 -> 2; matrix products, arithmetic and copies ran while one was open for 3% -> 8% of each run, Pallas kernels for 0% -> 0%
where the time goes in v1:
time: 202 us; the launch traced here: 201 us
  waiting for transfers between devices  107 us (53%)
  blocking collectives  39.9 us (20%)
  between operations  16.6 us (8%)
  other arithmetic  11.5 us (6%)
  matrix products  11.1 us (5%)
  local copies, waits for them, and re-layouts  9.49 us (5%)
  starting transfers between devices  5.88 us (3%)
    ppermute x2, waiting for transfers between devices, _press_table(): all_values = lax.ppermute(y2, across, right_arr)  106 us
    psum x1, blocking collectives, body(): trace_p, trace_c = lax.psum((trace_p_part, trace_c_part), ('row', 'col'))  39.9 us
    dot_general x1, matrix products, body(): jnp.dot(bind_clusters(density, 'col', 1), column_panel, preferred_element...  11.1 us
    ppermute x2, starting transfers between devices, _press_table(): all_values = lax.ppermute(y2, across, right_arr)  5.84 us
    reshape x1, local copies, waits for them, and re-layouts, expand_blocks(): return grid.reshape(block_rows * width, block_cols * width)  4.85 us
  transfers between devices with their start and end apart: 3, of which 2 were waited for; matrix products, arithmetic and copies ran while one was open for 8% of the time, Pallas kernels for 0%

profile of v1, /device:TPU:0, one launch (start us, length us, event | category | flops | bytes accessed | tf_op | source)
XLA Modules:
  0.0 201.5 jit_solution(17020744679432661704)
XLA Ops:
  7.2 0.0 all-gather.2.cloned.1.call-start
  7.2 0.7 all-gather.2.cloned.1.call-update
  7.9 1.5 copy.4
  9.4 3.1 %collective-permute-start = (bf16[1,512,1024]{1,2,0:T(8,128)(2,1)S(1)}, bf16[1,512,1024]{1,2,0:T(8,128)(2,1)}, u32[]{:S(2)}, u32[]{:S(2)}) collective-permute-start(bf16[1,512,1024]{1,2,0:T(8,128)(2,1)S(1)} %bitcast.12), channel_id=1, source_target_pairs={{0,1},{1,0},{2,3},{3,2},{4,5},{5,4},{6,7},{7,6},{8,9},{9,8},{10,11... | collective-permute-start | bytes 3145736 | tf_op jit(solution)/shard_map/ppermute | solution.py:23
  12.5 23.3 %collective-permute-done = bf16[1,512,1024]{1,2,0:T(8,128)(2,1)} collective-permute-done((bf16[1,512,1024]{1,2,0:T(8,128)(2,1)S(1)}, bf16[1,512,1024]{1,2,0:T(8,128)(2,1)}, u32[]{:S(2)}, u32[]{:S(2)}) %collective-permute-start) | collective-permute-done | bytes 1048608 | tf_op jit(solution)/shard_map/ppermute | solution.py:23
  35.8 1.4 broadcast_select_fusion.3
  37.1 0.0 copy-start.2
  37.1 1.5 pad_maximum_fusion.1
  38.6 2.8 %collective-permute-start.1 = (bf16[2,512,1024]{1,2,0:T(8,128)(2,1)}, bf16[2,512,1024]{1,2,0:T(8,128)(2,1)}, u32[]{:S(2)}, u32[]{:S(2)}) collective-permute-start(bf16[2,512,1024]{1,2,0:T(8,128)(2,1)} %pad_maximum_fusion.1), channel_id=1, source_target_pairs={{0,2},{1,3},{2,0},{3,1},{4,6},{5,7},{6,4},{7,5},{8,10},{9,11},{10,... | collective-permute-start | bytes 6291464 | tf_op jit(solution)/shard_map/ppermute | solution.py:23
  41.4 0.0 copy-done.2
  41.4 2.3 %broadcast_in_dim.18 = f32[8,64,16,64]{3,2,1,0:T(8,128)} broadcast(f32[8,16]{1,0:T(8,128)S(1)} %convert_element_type.10), dimensions={0,2} | broadcast | bytes 2097664 | tf_op jit(solution)/shard_map/broadcast_in_dim | solution.py:32
  43.7 4.8 %reshape.20 = f32[512,1024]{1,0:T(8,128)} reshape(f32[8,64,16,64]{3,2,1,0:T(8,128)} %broadcast_in_dim.18) | data formatting | bytes 4194304 | tf_op jit(solution)/shard_map/reshape | solution.py:35
  48.5 83.1 %collective-permute-done.1 = bf16[2,512,1024]{1,2,0:T(8,128)(2,1)} collective-permute-done((bf16[2,512,1024]{1,2,0:T(8,128)(2,1)}, bf16[2,512,1024]{1,2,0:T(8,128)(2,1)}, u32[]{:S(2)}, u32[]{:S(2)}) %collective-permute-start.1) | collective-permute-done | bytes 2097184 | tf_op jit(solution)/shard_map/ppermute | solution.py:23
  131.6 1.9 broadcast_select_fusion.1
  133.5 0.0 copy-start
  133.5 0.0 copy-start.1
  133.5 2.4 %pad_maximum_fusion = bf16[4,512,1024]{1,2,0:T(8,128)(2,1)} fusion(bf16[2,512,1024]{1,2,0:T(8,128)(2,1)S(1)} %get-tuple-element.7, bf16[2,512,1024]{1,2,0:T(8,128)(2,1)S(1)} %get-tuple-element.6), kind=kLoop, calls=%fused_computation | loop fusion | flops 2097152 | bytes 8388608 | tf_op jit(solution)/shard_map/concatenate | solution.py:25
  135.9 0.0 all-gather.2.cloned.1.call-done
  135.9 0.0 copy-done
  135.9 0.8 copy-done.1
  136.8 11.1 %fusion.5 = (f32[]{:T(128)}, f32[]{:T(128)}, f32[512,1024]{1,0:T(8,128)}) fusion(f32[512,1024]{1,0:T(8,128)S(1)} %copy-done.1, s32[1024]{0:T(1024)S(1)} %iota_add_fusion, s32[512]{0:T(512)S(1)} %iota_add_fusion.1, bf16[512,1024]{1,0:T(8,128)(2,1)S(1)} %copy-done, bf16[512,4096]{0,1:T(8,128)(2,1)} %bitcast.13, bf16[4096,1024]{1,0:T(8,128)(2,1)} %all-gather.2.cloned.1.call-done), kind=kOutput, calls=%fused_computation.9 | convolution fusion | flops 4298637312 | bytes 17831944 | tf_op jit(solution)/shard_map/dot_general | solution.py:53
  147.9 39.9 %all-reduce = (f32[]{:T(128)}, f32[]{:T(128)}) all-reduce(f32[]{:T(128)} %get-tuple-element.3, f32[]{:T(128)} %get-tuple-element.2), channel_id=1, replica_groups=mesh['row'=8,'col'=4] {'row','col'}, use_global_device_ids=true, to_apply=%region_1.2 | all-reduce | flops 2 | bytes 16 | tf_op jit(solution)/shard_map/psum | solution.py:58
  190.3 3.2 %fusion.3 = bf16[512,1024]{1,0:T(8,128)(2,1)} fusion(f32[512,1024]{1,0:T(8,128)S(1)} %copy-done.1, bf16[512,1024]{1,0:T(8,128)(2,1)S(1)} %copy-done, f32[512,1024]{1,0:T(8,128)} %get-tuple-element.10, pred[]{:T(512)S(6)} %gt.3), kind=kLoop, calls=%fused_computation.7 | loop fusion | flops 3670016 | bytes 6291457 | tf_op jit(solution)/shard_map/convert_element_type | solution.py:64
  193.4 1.2 maximum_multiply_fusion
  (3 shorter events, 0.0 us)
Async XLA Ops:
  7.2 128.8 %all-gather.2.cloned.1.call-start = ((), (), s32[]{:S(2)}) async-start(), calls=%async_computation | async-start | bytes 9437184 | tf_op jit(solution)/shard_map/all_gather | solution.py:41
  9.4 26.4 %collective-permute-start = (bf16[1,512,1024]{1,2,0:T(8,128)(2,1)S(1)}, bf16[1,512,1024]{1,2,0:T(8,128)(2,1)}, u32[]{:S(2)}, u32[]{:S(2)}) collective-permute-start(bf16[1,512,1024]{1,2,0:T(8,128)(2,1)S(1)} %bitcast.12), channel_id=1, source_target_pairs={{0,1},{1,0},{2,3},{3,2},{4,5},{5,4},{6,7},{7,6},{8,9},{9,8},{10,11... | collective-permute-start | bytes 3145736 | tf_op jit(solution)/shard_map/ppermute | solution.py:23
  37.1 4.3 %copy-start.2 = (s32[8,16]{1,0:T(8,128)S(1)}, s32[8,16]{1,0:T(8,128)}, u32[]{:S(2)}) copy-start(s32[8,16]{1,0:T(8,128)} %param.3) | copy-start | bytes 1540
  38.6 93.0 %collective-permute-start.1 = (bf16[2,512,1024]{1,2,0:T(8,128)(2,1)}, bf16[2,512,1024]{1,2,0:T(8,128)(2,1)}, u32[]{:S(2)}, u32[]{:S(2)}) collective-permute-start(bf16[2,512,1024]{1,2,0:T(8,128)(2,1)} %pad_maximum_fusion.1), channel_id=1, source_target_pairs={{0,2},{1,3},{2,0},{3,1},{4,6},{5,7},{6,4},{7,5},{8,10},{9,11},{10,... | collective-permute-start | bytes 6291464 | tf_op jit(solution)/shard_map/ppermute | solution.py:23
  133.5 2.5 %copy-start = (bf16[512,1024]{1,0:T(8,128)(2,1)S(1)}, bf16[512,1024]{1,0:T(8,128)(2,1)}, u32[]{:S(2)}) copy-start(bf16[512,1024]{1,0:T(8,128)(2,1)} %param.2) | copy-start | bytes 3145732
  133.5 3.3 %copy-start.1 = (f32[512,1024]{1,0:T(8,128)S(1)}, f32[512,1024]{1,0:T(8,128)}, u32[]{:S(2)}) copy-start(f32[512,1024]{1,0:T(8,128)} %reshape.20) | copy-start | bytes 6291460
Sparse Core Ops, SparseCore 0:
  9.9 57.0 all-gather.1
